TPU v7x, 256 devices: a whole 4x4x8 slice. The times are simulated.
256 devices in a mesh: section: 16 (over y_hi, x, core), expert: 16 (over z, y_lo).
Axes of the slice: x: 4, y: 4 (y_hi: 2, y_lo: 2; y = y_hi * 2 + y_lo), z: 8, core: 2. Of those that a mesh axis runs over, the one named last changes fastest.
Arguments:
- cotangent: bfloat16 [16, 2048, 4096], P('section', 'expert'), may hold values from -6 to 6
- routes: int32 [16, 2048, 2], P('section', 'expert'), may hold values from 0 to 15, all different within a row; in each aligned block of 64 rows (0 to 63, 64 to 127, ..., all dimensions but the last counted through in order) at most 16 rows name the same one
- gate_prob: float32 [16, 2048, 2], P('section', 'expert'), may hold values from 0.05 to 1
- hidden: bfloat16 [16, 16, 2, 16, 16, 1536], P('section', 'expert'), may hold values from -6 to 6
Outputs:
- grad_pair: bfloat16 [8, 16, 1536, 4096], P(None, 'expert', 'section')
Inputs may be any that keep to these rules, and one draw needn't show every extreme that they name: `routes`: each row names 2 different experts. In each aligned block of 64 rows (one micro-batch of one device) no expert is named by more than 16 rows.
All inputs are finite; a program needn't handle non-finite values.
Results may differ from a plain program's by a relative error of at most 0.0059.
Values may be sent and summed in bfloat16 or wider, within the bound.
A program may use at most 128 MiB of HBM per device.

v0:
```python
from functools import partial
import jax
import jax.numpy as jnp
from jax import lax
from jax.sharding import PartitionSpec as P


def slot_index(route_blk, experts_total):
    labels = jnp.arange(experts_total, dtype=jnp.int32)
    hits = (route_blk[:, :, None] == labels).astype(jnp.int32)
    per_token = jnp.sum(hits, axis=1)
    before = jnp.cumsum(per_token, axis=0) - per_token
    return jnp.sum(hits * before[:, None, :], axis=2)


def pack_block(cot_blk, route_blk, prob_blk, experts_total, capacity):
    width = cot_blk.shape[1]
    slots = slot_index(route_blk, experts_total)
    flat = (route_blk * capacity + slots).reshape(-1)
    weighted = (prob_blk[:, :, None] * cot_blk[:, None, :].astype(jnp.float32)).astype(jnp.bfloat16)
    empty = jnp.zeros((experts_total * capacity, width), jnp.bfloat16)
    return empty.at[flat].set(weighted.reshape(-1, width)).reshape(experts_total, capacity, width)


def rows_product(acts, arrived):
    return lax.dot_general(
        acts, arrived, (((0,), (0,)), ((), ())), preferred_element_type=jnp.float32
    )


def pair_add(pieces, half):
    lower = pieces[:half].astype(jnp.float32)
    upper = jnp.flip(pieces[half:], 0).astype(jnp.float32)
    return (lower + upper).astype(jnp.bfloat16)


def local(cotangent, routes, gate_prob, hidden):
    n_section = lax.axis_size("section")
    half = n_section // 2
    mb_count = hidden.shape[2]
    sources = hidden.shape[3]
    capacity = hidden.shape[4]
    ff_width = hidden.shape[5]
    width = cotangent.shape[2]
    top_count = routes.shape[2]
    tok_block = cotangent.shape[1] // mb_count
    cot_blocks = cotangent.reshape(mb_count, tok_block, width)
    route_blocks = routes.reshape(mb_count, tok_block, top_count)
    prob_blocks = gate_prob.reshape(mb_count, tok_block, top_count)
    packer = partial(pack_block, experts_total=sources, capacity=capacity)
    packed = jax.vmap(packer)(cot_blocks, route_blocks, prob_blocks)
    acts = hidden.reshape(mb_count * sources * capacity, ff_width)
    arrived = lax.all_to_all(packed, "expert", split_axis=1, concat_axis=1, tiled=True)
    rows = arrived.reshape(mb_count * sources * capacity, width)
    part = rows_product(acts, rows).astype(jnp.bfloat16)
    pieces = lax.all_to_all(part[None], "section", split_axis=1, concat_axis=0, tiled=True)
    result = pair_add(pieces, half)
    return result[:, None]


def solution(mesh):
    return jax.shard_map(
        local,
        mesh=mesh,
        in_specs=(
            P("section", "expert", None),
            P("section", "expert", None),
            P("section", "expert", None),
            P("section", "expert", None, None, None, None),
        ),
        out_specs=P(None, "expert", "section", None),
        check_vma=False,
    )
```

profile of v0, /device:TPU:1, one launch (start us, length us, event | category | flops | bytes accessed | tf_op | source)
XLA Modules:
  0.0 582.4 jit_solution(12022639161730682039)
XLA Ops:
  0.0 0.0 copy-start
  0.0 0.9 eq.15
  0.9 0.7 broadcast_multiply_fusion
  1.6 0.1 copy.30
  1.7 0.1 reduce_window_sum.11
  1.8 0.1 copy.32
  1.9 0.1 copy.33
  2.0 0.1 reduce_sum.22
  2.1 0.1 copy.28
  2.2 0.1 mul.45
  2.4 5.3 mul.50
  7.7 0.0 copy-start.3
  7.7 6.1 %mul.51 = f32[2,128,4096]{2,1,0:T(8,128)} reshape(f32[2,64,2,4096]{3,2,1,0:T(2,128)} %mul.50) | data formatting | bytes 8388608 | tf_op jit(solution)/shard_map/vmap()/mul | solution.py:20
  13.8 0.0 copy-done.3
  13.8 0.1 copy.34
  13.9 0.1 mul.48
  14.1 4.0 multiply_convert_fusion
  18.1 2.5 broadcast_in_dim.12
  20.6 66.4 %scatter_fusion = bf16[2,256,4096]{2,1,0:T(8,128)(2,1)} fusion(bf16[2,256,4096]{2,1,0:T(8,128)(2,1)} %broadcast_in_dim.12, s32[256]{0:T(256)S(1)} %fusion.5, bf16[256,4096]{1,0:T(8,128)(2,1)} %bitcast.36), kind=kCustom, calls=%fused_computation | custom fusion | bytes 6293504 | tf_op jit(solution)/shard_map/vmap()/scatter | solution.py:22
  87.0 2.5 copy.35
  89.5 104.1 %all_to_all.17 = bf16[2,16,16,4096]{3,2,0,1:T(8,128)(2,1)S(1)} all-to-all(bf16[2,16,16,4096]{3,2,0,1:T(8,128)(2,1)S(1)} %copy.35), channel_id=1, replica_groups=mesh['section'=16,'expert'=16] {'expert'}, dimensions={1} | all-to-all | bytes 8388608 | tf_op jit(solution)/shard_map/all_to_all | solution.py:53
  193.6 0.5 copy.36
  194.1 0.0 copy-done
  194.1 9.7 %fusion = bf16[1,1536,4096]{1,2,0:T(8,128)(2,1)} fusion(bf16[512,4096]{1,0:T(8,128)(2,1)S(1)} %bitcast.37, bf16[512,1536]{1,0:T(8,128)(2,1)S(1)} %bitcast.29), kind=kOutput, calls=%fused_computation.2 | convolution fusion | flops 6448742400 | bytes 18350080 | tf_op jit(solution)/shard_map/dot_general | solution.py:26
  203.8 54.3 %copy.37 = bf16[1,1536,4096]{2,0,1:T(2,128)(2,1)} copy(bf16[1,1536,4096]{1,2,0:T(8,128)(2,1)} %fusion) | data formatting | bytes 25165824 | tf_op jit(solution)/shard_map/broadcast_in_dim | solution.py:56
  258.1 0.5 broadcast.51
  258.6 77.6 %reduce = bf16[1536,4096]{1,0:T(8,128)(2,1)} reduce(bf16[1536,1,4096]{2,1,0:T(2,128)(2,1)} %bitcast.33, bf16[]{:T(256)} %broadcast.51), dimensions={1}, to_apply=%bitcast.25.reduce_sub_computation | reduce | bytes 25165826
  336.2 17.6 %reshape.86 = bf16[16,2,196608]{2,1,0:T(2,128)(2,1)} reshape(bf16[1536,4096]{1,0:T(8,128)(2,1)} %reduce) | data formatting | bytes 25165824
  353.8 149.8 %all_to_all.18 = bf16[16,2,196608]{2,1,0:T(2,128)(2,1)} all-to-all(bf16[16,2,196608]{2,1,0:T(2,128)(2,1)} %reshape.86), channel_id=1, replica_groups=mesh['section'=16,'expert'=16] {'section'}, dimensions={0} | all-to-all | bytes 25165824 | tf_op jit(solution)/shard_map/all_to_all | solution.py:56
  503.6 20.6 %reshape.87 = bf16[1536,1,4096]{2,1,0:T(2,128)(2,1)} reshape(bf16[16,2,196608]{2,1,0:T(2,128)(2,1)} %all_to_all.18) | data formatting | bytes 25165824
  524.2 0.0 copy-start.2
  524.2 15.5 %slice.16 = bf16[1,768,4096]{2,0,1:T(2,128)(2,1)} slice(bf16[1,1536,4096]{2,0,1:T(2,128)(2,1)} %bitcast.30), slice={[0:1], [768:1536], [0:4096]} | slice | bytes 12582912 | tf_op jit(solution)/shard_map/slice | solution.py:33
  539.7 0.7 copy-done.2
  540.4 17.1 %copy.40 = bf16[1,1536,4096]{2,1,0:T(8,128)(2,1)} copy(bf16[1,1536,4096]{2,0,1:T(2,128)(2,1)S(1)} %bitcast.31) | data formatting | bytes 25165824
  557.5 14.4 %copy.41 = bf16[1,768,4096]{2,1,0:T(8,128)(2,1)} copy(bf16[1,768,4096]{2,0,1:T(2,128)(2,1)} %slice.16) | data formatting | bytes 12582912
  571.9 0.0 copy-start.1
  571.9 10.5 %fusion.2 = bf16[8,1,96,4096]{3,2,1,0:T(8,128)(2,1)} fusion(bf16[1,16,96,4096]{3,2,1,0:T(8,128)(2,1)} %bitcast.34, bf16[8,96,4096]{2,1,0:T(8,128)(2,1)} %bitcast.35), kind=kLoop, calls=%fused_computation.5 | loop fusion | flops 12582912 | bytes 18874368 | tf_op jit(solution)/shard_map/broadcast_in_dim | solution.py:58
  582.4 0.0 copy-done.1
  (5 shorter events, 0.1 us)
Async XLA Ops:
  0.0 194.1 %copy-start = (bf16[1,1,2,16,16,1536]{5,4,3,2,1,0:T(8,128)(2,1)S(1)}, bf16[1,1,2,16,16,1536]{5,4,3,2,1,0:T(8,128)(2,1)}, u32[]{:S(2)}) copy-start(bf16[1,1,2,16,16,1536]{5,4,3,2,1,0:T(8,128)(2,1)} %param.7) | copy-start | bytes 4718596
  7.7 6.1 %copy-start.3 = (f32[1,128,2]{1,2,0:T(2,128)S(1)}, f32[1,128,2]{1,2,0:T(2,128)}, u32[]{:S(2)}) copy-start(f32[1,128,2]{1,2,0:T(2,128)} %param.6) | copy-start | bytes 3076
  524.2 16.2 %copy-start.2 = (bf16[1536,1,4096]{2,1,0:T(2,128)(2,1)S(1)}, bf16[1536,1,4096]{2,1,0:T(2,128)(2,1)}, u32[]{:S(2)}) copy-start(bf16[1536,1,4096]{2,1,0:T(2,128)(2,1)} %reshape.87) | copy-start | bytes 37748740
  571.9 10.6 %copy-start.1 = (bf16[1,1,2,16,16,1536]{5,4,3,2,1,0:T(8,128)(2,1)S(1)}, bf16[1,1,2,16,16,1536]{5,4,3,2,1,0:T(8,128)(2,1)}, u32[]{:S(2)}) copy-start(bf16[1,1,2,16,16,1536]{5,4,3,2,1,0:T(8,128)(2,1)} %param.7) | copy-start | bytes 4718596
where the time goes:
time: 586 us; the launch traced here: 582 us
  blocking collectives  254 us (43%)
  local copies, waits for them, and re-layouts  226 us (39%)
  other arithmetic  93 us (16%)
  matrix products  9.71 us (2%)
    all_to_all x1, blocking collectives, local(): lax.all_to_all(part[None], 'section', split_axis=1, concat_axis=0, tiled=...  150 us
    all_to_all x1, blocking collectives, local(): lax.all_to_all(packed, 'expert', split_axis=1, concat_axis=1, tiled=True)  104 us
    unnamed x1, other arithmetic  77.6 us
    unnamed x14, local copies, waits for them, and re-layouts  71 us
    scatter x1, local copies, waits for them, and re-layouts, pack_block(): empty.at[flat].set(weighted.reshape(-1, width))  66.4 us
    broadcast_in_dim x1, local copies, waits for them, and re-layouts, local(): part[None]  54.3 us
    slice x1, local copies, waits for them, and re-layouts, pair_add(): upper = jnp.flip(pieces[half:], 0).astype(jnp.float32)  15.5 us

commit v1 on v0

--- a/solution.py
+++ b/solution.py
@@ -53,7 +53,11 @@
     arrived = lax.all_to_all(packed, "expert", split_axis=1, concat_axis=1, tiled=True)
     rows = arrived.reshape(mb_count * sources * capacity, width)
     part = rows_product(acts, rows).astype(jnp.bfloat16)
-    pieces = lax.all_to_all(part[None], "section", split_axis=1, concat_axis=0, tiled=True)
+    part_2 = part[None]
+    count = lax.axis_size("section")
+    blocks = jnp.stack(jnp.split(part_2, count, axis=1), axis=0)
+    blocks = lax.all_to_all(blocks, "section", split_axis=0, concat_axis=0)
+    pieces = jnp.concatenate(blocks, axis=0)
     result = pair_add(pieces, half)
     return result[:, None]
 

time: 586 us -> 371 us (0.63)
  local copies, waits for them, and re-layouts: 226 us -> 93.9 us
  other arithmetic: 93 us -> 15.4 us
    unnamed x1 -> x0, other arithmetic: 77.6 us -> none
    unnamed x14 -> x22, local copies, waits for them, and re-layouts: 71 us -> 6.16 us
    broadcast_in_dim x1 -> x0, local copies, waits for them, and re-layouts: 54.3 us -> none  [local(): part[None]]
    slice x1, local copies, waits for them, and re-layouts: 15.5 us -> 3.03 us  [pair_add(): upper = jnp.flip(pieces[half:], 0).astype(jnp.float32)]
where the time goes in v1:
time: 371 us; the launch traced here: 370 us
  blocking collectives  254 us (68%)
  local copies, waits for them, and re-layouts  93.9 us (25%)
  other arithmetic  15.4 us (4%)
  matrix products  7.26 us (2%)
    all_to_all x1, blocking collectives, local(): blocks = lax.all_to_all(blocks, 'section', split_axis=0, concat_axis=0)  149 us
    all_to_all x1, blocking collectives, local(): lax.all_to_all(packed, 'expert', split_axis=1, concat_axis=1, tiled=True)  104 us
    scatter x1, local copies, waits for them, and re-layouts, pack_block(): empty.at[flat].set(weighted.reshape(-1, width))  66.4 us
    mul x3, local copies, waits for them, and re-layouts, pack_block(): prob_blk[:, :, None] * cot_blk[:, None, :].astype(jnp.float32)  11.5 us
    broadcast_in_dim x1, other arithmetic, local(): return result[:, None]  10.4 us

profile of v1, /device:TPU:1, one launch (start us, length us, event | category | flops | bytes accessed | tf_op | source)
XLA Modules:
  0.0 370.3 jit_solution(7911290514789984910)
XLA Ops:
  0.0 0.0 copy-start
  0.0 0.8 broadcast_multiply_fusion
  0.8 0.8 eq.15
  1.6 0.1 copy.27
  1.7 0.1 copy.25
  1.8 0.1 mul.45
  1.9 0.1 reduce_window_sum.11
  2.0 0.1 copy.29
  2.1 0.1 copy.30
  2.2 0.1 reduce_sum.22
  2.4 0.8 copy.31
  3.2 0.1 mul.48
  3.3 5.3 %mul.50 = f32[2,64,2,4096]{3,2,1,0:T(2,128)} broadcast(bf16[2,64,4096]{2,1,0:T(8,128)(2,1)} %bitcast.98), dimensions={0,1,3} | broadcast | bytes 5242880 | tf_op jit(solution)/shard_map/vmap()/mul | solution.py:20
  8.7 6.1 %mul.51 = f32[2,128,4096]{2,1,0:T(8,128)} reshape(f32[2,64,2,4096]{3,2,1,0:T(2,128)} %mul.50) | data formatting | bytes 8388608 | tf_op jit(solution)/shard_map/vmap()/mul | solution.py:20
  14.7 4.0 %multiply_convert_fusion = bf16[2,128,4096]{2,1,0:T(8,128)(2,1)} fusion(f32[2,128,4096]{2,1,0:T(8,128)} %mul.51, f32[2,128]{1,0:T(2,128)S(1)} %mul.48), kind=kLoop, calls=%fused_computation.8 | loop fusion | flops 2097152 | bytes 6292480 | tf_op jit(solution)/shard_map/vmap()/convert_element_type | solution.py:20
  18.7 2.5 broadcast_in_dim.12
  21.2 66.4 %scatter_fusion = bf16[2,256,4096]{2,1,0:T(8,128)(2,1)} fusion(bf16[2,256,4096]{2,1,0:T(8,128)(2,1)} %broadcast_in_dim.12, s32[256]{0:T(256)S(1)} %fusion.21, bf16[256,4096]{1,0:T(8,128)(2,1)} %bitcast.96), kind=kCustom, calls=%fused_computation | custom fusion | bytes 6293504 | tf_op jit(solution)/shard_map/vmap()/scatter | solution.py:22
  87.7 2.5 copy.32
  90.1 104.3 %all_to_all.10 = bf16[2,16,16,4096]{3,2,0,1:T(8,128)(2,1)S(1)} all-to-all(bf16[2,16,16,4096]{3,2,0,1:T(8,128)(2,1)S(1)} %copy.32), channel_id=1, replica_groups=mesh['section'=16,'expert'=16] {'expert'}, dimensions={1} | all-to-all | bytes 8388608 | tf_op jit(solution)/shard_map/all_to_all | solution.py:53
  194.4 0.3 copy.33
  194.7 0.0 copy-done
  194.7 7.3 %fusion = bf16[1,1536,4096]{2,1,0:T(8,128)(2,1)S(1)} fusion(bf16[512,4096]{1,0:T(8,128)(2,1)S(1)} %bitcast.97, bf16[512,1536]{1,0:T(8,128)(2,1)S(1)} %bitcast.93), kind=kOutput, calls=%fused_computation.2 | convolution fusion | flops 6448742400 | bytes 18350080 | tf_op jit(solution)/shard_map/dot_general | solution.py:26
  202.0 0.1 fusion.18
  202.0 0.1 fusion.17
  202.1 0.1 fusion.16
  202.1 0.1 fusion.15
  202.2 0.1 fusion.14
  202.3 0.1 fusion.13
  202.3 0.1 fusion.12
  202.4 0.1 fusion.11
  202.4 0.1 fusion.10
  202.5 0.1 fusion.9
  202.6 0.1 fusion.8
  202.6 0.1 fusion.7
  202.7 0.1 fusion.6
  202.7 0.1 fusion.5
  202.8 0.1 fusion.4
  202.9 0.1 fusion.3
  202.9 149.4 %all_to_all.11 = bf16[16,1,96,4096]{3,2,1,0:T(8,128)(2,1)S(1)} all-to-all(bf16[16,1,96,4096]{3,2,1,0:T(8,128)(2,1)S(1)} %fusion.3), channel_id=1, replica_groups=mesh['section'=16,'expert'=16] {'section'}, dimensions={0} | all-to-all | bytes 25165824 | tf_op jit(solution)/shard_map/all_to_all | solution.py:59
  352.3 0.0 copy-start.2
  352.3 4.6 %copy-done.2 = bf16[16,1,96,4096]{3,2,1,0:T(8,128)(2,1)} copy-done((bf16[16,1,96,4096]{3,2,1,0:T(8,128)(2,1)}, bf16[16,1,96,4096]{3,2,1,0:T(8,128)(2,1)S(1)}, u32[]{:S(2)}) %copy-start.2) | copy-done | bytes 12582936
  356.9 0.0 copy-start.1
  356.9 3.0 slice_bitcast_fusion
  359.9 10.4 %fusion.2 = bf16[8,1,96,4096]{3,2,1,0:T(8,128)(2,1)} fusion(bf16[16,1,96,4096]{3,2,0,1:T(8,128)(2,1)} %bitcast.95, bf16[8,96,4096]{2,1,0:T(8,128)(2,1)} %slice_bitcast_fusion), kind=kLoop, calls=%fused_computation.5 | loop fusion | flops 12582912 | bytes 18874368 | tf_op jit(solution)/shard_map/broadcast_in_dim | solution.py:62
  370.3 0.0 copy-done.1
  (5 shorter events, 0.1 us)
Async XLA Ops:
  0.0 194.7 %copy-start = (bf16[1,1,2,16,16,1536]{5,4,3,2,1,0:T(8,128)(2,1)S(1)}, bf16[1,1,2,16,16,1536]{5,4,3,2,1,0:T(8,128)(2,1)}, u32[]{:S(2)}) copy-start(bf16[1,1,2,16,16,1536]{5,4,3,2,1,0:T(8,128)(2,1)} %param.7) | copy-start | bytes 4718596
  352.3 4.6 %copy-start.2 = (bf16[16,1,96,4096]{3,2,1,0:T(8,128)(2,1)}, bf16[16,1,96,4096]{3,2,1,0:T(8,128)(2,1)S(1)}, u32[]{:S(2)}) copy-start(bf16[16,1,96,4096]{3,2,1,0:T(8,128)(2,1)S(1)} %all_to_all.11) | copy-start | bytes 37748740
  356.9 13.5 %copy-start.1 = (bf16[1,1,2,16,16,1536]{5,4,3,2,1,0:T(8,128)(2,1)S(1)}, bf16[1,1,2,16,16,1536]{5,4,3,2,1,0:T(8,128)(2,1)}, u32[]{:S(2)}) copy-start(bf16[1,1,2,16,16,1536]{5,4,3,2,1,0:T(8,128)(2,1)} %param.7) | copy-start | bytes 4718596
